TPU v7x, 256 devices: a whole 4x4x8 slice. The times are simulated.
256 devices in a mesh: seq: 64 (over y, z, core), tp: 4 (over x).
Axes of the slice: x: 4, y: 4, z: 8, core: 2. Of those that a mesh axis runs over, the one named last changes fastest.
Arguments:
- inputs: bfloat16 [4, 4, 1024], P(None, None, 'tp'), may hold values from -64 to 64
- attention_gain: bfloat16 [1024], replicated, may hold values from 0.099609375 to 1.8984375
- forward_gain: bfloat16 [1024], replicated, may hold values from 0.099609375 to 1.8984375
- query_weight: bfloat16 [1024, 1024], P(None, 'tp'), may hold values from -0.1875 to 0.1875
- key_weight: bfloat16 [1024, 1024], P(None, 'tp'), may hold values from -0.1875 to 0.1875
- value_weight: bfloat16 [1024, 1024], P(None, 'tp'), may hold values from -0.1875 to 0.1875
- output_weight: bfloat16 [1024, 1024], P('tp'), may hold values from -0.1875 to 0.1875
- gate_weight: bfloat16 [1024, 4096], P(None, 'tp'), may hold values from -0.1875 to 0.1875
- up_weight: bfloat16 [1024, 4096], P(None, 'tp'), may hold values from -0.1875 to 0.1875
- down_weight: bfloat16 [4096, 1024], P('tp'), may hold values from -0.09375 to 0.09375
- variate_bias: float32 [2, 16], replicated, may hold values from -256 to 256
- cache_keys: bfloat16 [4, 32768, 1024], P(None, 'seq', 'tp'), may hold values from -15 to 15
- cache_values: bfloat16 [4, 32768, 1024], P(None, 'seq', 'tp'), may hold values from -12 to 12
- cache_variates: int32 [4, 32768], P(None, 'seq'), may hold values from 0 to 7
- cache_mask: int32 [4, 32768], P(None, 'seq'), may hold values 0 or 1
- cache_lengths: int32 [4], replicated, may hold values from 1 to 32768, as said below
- fresh_flags: int32 [4], replicated, may hold values 0 or 1
- new_variates: int32 [4, 4], replicated, may hold values from 0 to 7
- new_times: int32 [4, 4], replicated, may hold values from 0 to 32771
Outputs:
- hidden_states: bfloat16 [4, 4, 1024], P(None, None, 'tp')
- new_keys: bfloat16 [4, 4, 1024], P(None, None, 'tp')
- new_values: bfloat16 [4, 4, 1024], P(None, None, 'tp')
Inputs may be any that keep to these rules, and one draw needn't show every extreme that they name: `cache_lengths`: some request has exactly 32768 filled positions.
All inputs are finite; a program needn't handle non-finite values. No bound on the sum of `cache_mask` on one device may be relied on, other than what follows from the above.
Results may differ from a plain program's by a relative error of at most 0.014.
Values may be sent and summed in bfloat16 or wider, within the bound.
A program may use at most 64 MiB of HBM per device.

v0:
```python
import math
import jax
import jax.numpy as jnp
from jax import lax
from jax.sharding import PartitionSpec as P

D = 1024
HEAD_DIM = 64
STEPS = 4
epsilon = 1e-05


def rotated(blocks, times):
    half = blocks.shape[-1] // 2
    ladder = jnp.arange(half, dtype=jnp.float32) * (2.0 / blocks.shape[-1])
    inverse = jnp.exp(-math.log(10000.0) * ladder)
    angles = times.astype(jnp.float32)[:, None] * inverse[None, :]
    cosine = jnp.cos(angles)[:, None, :]
    sine = jnp.sin(angles)[:, None, :]
    first = blocks[..., :half]
    second = blocks[..., half:]
    return jnp.concatenate(
        [first * cosine - second * sine, second * cosine + first * sine], axis=-1
    )


def join_parts(earlier, later):
    peak = jnp.maximum(earlier[0], later[0])
    factor_one = jnp.exp(earlier[0] - peak)
    factor_two = jnp.exp(later[0] - peak)
    totals = earlier[1] * factor_one + later[1] * factor_two
    repeat_by = earlier[2].shape[-1] // earlier[0].shape[-1]
    sums = earlier[2] * jnp.repeat(factor_one, repeat_by, axis=1) + later[2] * jnp.repeat(
        factor_two, repeat_by, axis=1
    )
    return (peak, totals, sums)


def on_device(
    inputs,
    attention_gain,
    forward_gain,
    query_weight,
    key_weight,
    value_weight,
    output_weight,
    gate_weight,
    up_weight,
    down_weight,
    variate_bias,
    cache_keys,
    cache_values,
    cache_variates,
    cache_mask,
    cache_lengths,
    fresh_flags,
    new_variates,
    new_times,
):
    local_width = query_weight.shape[1]
    local_heads = local_width // HEAD_DIM
    requests = inputs.shape[0]
    columns = inputs.shape[2]
    span = cache_keys.shape[1]
    scale = 1.0 / math.sqrt(HEAD_DIM)
    column_start = lax.axis_index("tp") * columns
    head_start = lax.axis_index("tp") * local_heads
    bias_local = lax.dynamic_slice_in_dim(variate_bias, head_start, local_heads, 1)
    same_bias = bias_local[0]
    other_bias = bias_local[1]
    positions = lax.axis_index("seq") * span + jnp.arange(span, dtype=jnp.int32)
    usable = (
        (positions[None, :] < cache_lengths[:, None])
        & (cache_mask == 1)
        & (fresh_flags[:, None] == 0)
    )
    key_blocks = cache_keys.reshape(requests, span, local_heads, HEAD_DIM)
    value_blocks = cache_values.reshape(requests, span, local_heads, HEAD_DIM)
    gain_first = attention_gain.astype(jnp.float32)[None, :]
    gain_second = forward_gain.astype(jnp.float32)[None, :]
    gain_first_local = lax.dynamic_slice_in_dim(gain_first, column_start, columns, 1)
    gain_second_local = lax.dynamic_slice_in_dim(gain_second, column_start, columns, 1)
    hidden_list = []
    key_list = []
    value_list = []
    for step_index in range(STEPS):
        current_low = inputs[:, step_index, :]
        current_local = current_low.astype(jnp.float32)
        square_sum = lax.psum(jnp.sum(current_local * current_local, axis=1), "tp")
        inverse_rms = lax.rsqrt(square_sum / D + epsilon)
        normed_local = (current_local * inverse_rms[:, None] * gain_first_local).astype(
            jnp.bfloat16
        )
        normed = lax.all_gather(normed_local, "tp", axis=1, tiled=True)
        query_full = jnp.dot(normed, query_weight, preferred_element_type=jnp.float32)
        key_full = jnp.dot(normed, key_weight, preferred_element_type=jnp.float32)
        value_full = jnp.dot(normed, value_weight, preferred_element_type=jnp.float32)
        times_now = new_times[:, step_index]
        queries_now = rotated(
            query_full.reshape(requests, local_heads, HEAD_DIM), times_now
        ).astype(jnp.bfloat16)
        keys_now = rotated(key_full.reshape(requests, local_heads, HEAD_DIM), times_now).astype(
            jnp.bfloat16
        )
        values_now = value_full.reshape(requests, local_heads, HEAD_DIM).astype(jnp.bfloat16)
        key_list.append(keys_now)
        value_list.append(values_now)
        variate_now = new_variates[:, step_index]
        same_cache = cache_variates == variate_now[:, None]
        scores = (
            jnp.einsum("rhe,rche->rhc", queries_now, key_blocks, preferred_element_type=jnp.float32)
            * scale
        )
        scores = scores + jnp.where(
            same_cache[:, None, :], same_bias[None, :, None], other_bias[None, :, None]
        )
        scores = jnp.where(usable[:, None, :], scores, -1e30)
        local_peak = jnp.max(scores, axis=2)
        raw = jnp.where(usable[:, None, :], jnp.exp(scores - local_peak[:, :, None]), 0.0)
        local_total = jnp.sum(raw, axis=2)
        local_sum = jnp.einsum(
            "rhc,rche->rhe",
            raw.astype(jnp.bfloat16),
            value_blocks,
            preferred_element_type=jnp.float32,
        ).reshape(requests, local_width)
        peak_all = lax.pmax(local_peak, "seq")
        factor = jnp.exp(local_peak - peak_all)
        totals_all, sums_all = lax.psum(
            (local_total * factor, local_sum * jnp.repeat(factor, HEAD_DIM, axis=1)), "seq"
        )
        merged = (peak_all, totals_all, sums_all)
        fresh_keys = jnp.stack(key_list, axis=1)
        fresh_values = jnp.stack(value_list, axis=1)
        same_new = new_variates[:, : step_index + 1] == variate_now[:, None]
        new_scores = (
            jnp.einsum("rhe,rshe->rhs", queries_now, fresh_keys, preferred_element_type=jnp.float32)
            * scale
        )
        new_scores = new_scores + jnp.where(
            same_new[:, None, :], same_bias[None, :, None], other_bias[None, :, None]
        )
        new_peak = jnp.max(new_scores, axis=2)
        new_raw = jnp.exp(new_scores - new_peak[:, :, None])
        new_total = jnp.sum(new_raw, axis=2)
        new_sum = jnp.einsum(
            "rhs,rshe->rhe",
            new_raw.astype(jnp.bfloat16),
            fresh_values,
            preferred_element_type=jnp.float32,
        ).reshape(requests, local_width)
        joined = join_parts(merged, (new_peak, new_total, new_sum))
        attention = (joined[2] / jnp.repeat(joined[1], HEAD_DIM, axis=1)).astype(jnp.bfloat16)
        partial_out = jnp.dot(attention, output_weight, preferred_element_type=jnp.float32)
        projected_local = lax.psum_scatter(partial_out, "tp", scatter_dimension=1, tiled=True)
        middle_local = (current_local + projected_local).astype(jnp.bfloat16).astype(jnp.float32)
        middle_sum = lax.psum(jnp.sum(middle_local * middle_local, axis=1), "tp")
        second_rms = lax.rsqrt(middle_sum / D + epsilon)
        normed_two_local = (middle_local * second_rms[:, None] * gain_second_local).astype(
            jnp.bfloat16
        )
        normed_two = lax.all_gather(normed_two_local, "tp", axis=1, tiled=True)
        gate_part = jnp.dot(normed_two, gate_weight, preferred_element_type=jnp.float32)
        up_part = jnp.dot(normed_two, up_weight, preferred_element_type=jnp.float32)
        activated = (jax.nn.silu(gate_part) * up_part).astype(jnp.bfloat16)
        down_part = jnp.dot(activated, down_weight, preferred_element_type=jnp.float32)
        forward = lax.psum_scatter(down_part, "tp", scatter_dimension=1, tiled=True)
        hidden_list.append((middle_local + forward).astype(jnp.bfloat16))
    hidden_states = jnp.stack(hidden_list, axis=1)
    new_keys = jnp.stack(key_list, axis=1).reshape(requests, STEPS, local_width)
    new_values = jnp.stack(value_list, axis=1).reshape(requests, STEPS, local_width)
    return (hidden_states, new_keys, new_values)


def solution(mesh):
    return jax.shard_map(
        on_device,
        mesh=mesh,
        in_specs=(
            P(None, None, "tp"),
            P(),
            P(),
            P(None, "tp"),
            P(None, "tp"),
            P(None, "tp"),
            P("tp", None),
            P(None, "tp"),
            P(None, "tp"),
            P("tp", None),
            P(),
            P(None, "seq", "tp"),
            P(None, "seq", "tp"),
            P(None, "seq"),
            P(None, "seq"),
            P(),
            P(),
            P(),
            P(),
        ),
        out_specs=(P(None, None, "tp"), P(None, None, "tp"), P(None, None, "tp")),
        check_vma=False,
    )
```

profile of v0, /device:TPU:8, one launch (start us, length us, event | category | flops | bytes accessed | tf_op | source)
XLA Modules:
  0.0 712.5 jit_solution(17226373592038998446)
XLA Ops:
  7.3 0.9 fusion.172
  8.7 10.5 %all-reduce.3 = (f32[4]{0:T(128)S(1)}, f32[4]{0:T(128)S(1)}, f32[4]{0:T(128)S(1)}, f32[4]{0:T(128)S(1)}) all-reduce(f32[4]{0:T(128)S(1)} %fusion.94, f32[4]{0:T(128)S(1)} %fusion.106, f32[4]{0:T(128)S(1)} %fusion.102, f32[4]{0:T(128)S(1)} %fusion.98), channel_id=1, replica_groups=mesh['seq'=64,'tp'=4] {'tp'}, use_global_device_ids=true, to_apply=%region_1.0 | all-reduce | flops 16 | bytes 128 | tf_op jit(solution)/shard_map/psum | solution.py:89
  19.2 0.8 dynamic-slice.6
  20.1 10.4 %all_gather.24 = bf16[4,1024]{1,0:T(4,128)(2,1)S(1)} all-gather(bf16[4,256]{1,0:T(4,128)(2,1)S(1)} %get-tuple-element.136), channel_id=1, replica_groups=mesh['seq'=64,'tp'=4] {'tp'}, dimensions={1}, use_global_device_ids=true | all-gather | bytes 10240 | tf_op jit(solution)/shard_map/all_gather | solution.py:94
  30.5 1.2 convolution_convert_fusion.3
  31.7 1.2 fusion.174
  32.9 10.5 %all_gather.26 = bf16[4,1024]{1,0:T(4,128)(2,1)S(1)} all-gather(bf16[4,256]{1,0:T(4,128)(2,1)S(1)} %get-tuple-element.137), channel_id=1, replica_groups=mesh['seq'=64,'tp'=4] {'tp'}, dimensions={1}, use_global_device_ids=true | all-gather | bytes 10240 | tf_op jit(solution)/shard_map/all_gather | solution.py:94
  43.4 1.2 convolution_convert_fusion.2
  44.6 1.2 fusion.177
  46.2 10.4 %all_gather.28 = bf16[4,1024]{1,0:T(4,128)(2,1)S(1)} all-gather(bf16[4,256]{1,0:T(4,128)(2,1)S(1)} %get-tuple-element.138), channel_id=1, replica_groups=mesh['seq'=64,'tp'=4] {'tp'}, dimensions={1}, use_global_device_ids=true | all-gather | bytes 10240 | tf_op jit(solution)/shard_map/all_gather | solution.py:94
  57.1 10.5 %all_gather.30 = bf16[4,1024]{1,0:T(4,128)(2,1)S(1)} all-gather(bf16[4,256]{1,0:T(4,128)(2,1)S(1)} %get-tuple-element.139), channel_id=1, replica_groups=mesh['seq'=64,'tp'=4] {'tp'}, dimensions={1}, use_global_device_ids=true | all-gather | bytes 10240 | tf_op jit(solution)/shard_map/all_gather | solution.py:94
  70.6 1.5 copy.47
  73.9 1.5 copy.48
  75.8 108.2 %all-reduce.1 = (f32[4,4]{1,0:T(4,128)S(1)}, f32[4,4]{1,0:T(4,128)S(1)}, f32[4,4]{1,0:T(4,128)S(1)}, f32[4,4]{1,0:T(4,128)S(1)}) all-reduce(f32[4,4]{1,0:T(4,128)S(1)} %get-tuple-element.78, f32[4,4]{1,0:T(4,128)S(1)} %get-tuple-element.125, f32[4,4]{1,0:T(4,128)S(1)} %get-tuple-element.123, ...), channel_id=1, replica_groups=mesh['seq'=64,'tp'=4] {'seq'}, use_global_device_ids=true, to_apply=%region_40.41 | all-reduce | flops 64 | bytes 512 | tf_op jit(solution)/shard_map/pmax | solution.py:127
  184.6 1.7 fusion.14
  186.3 1.6 fusion.16
  189.5 231.8 %all-reduce = (f32[4,4]{1,0:T(4,128)S(1)}, f32[4,256]{1,0:T(4,128)S(1)}, f32[4,4]{1,0:T(4,128)S(1)}, f32[4,256]{1,0:T(4,128)S(1)}, f32[4,4]{1,0:T(4,128)S(1)}, /...) all-reduce(f32[4,4]{1,0:T(4,128)S(1)} %get-tuple-element.70, ...), channel_id=1, replica_groups=mesh['seq'=64,'tp'=4] {'seq'}, use_global_device_ids=true, to_apply=%region_44.45 | all-reduce | flops 4160 | bytes 33280 | tf_op jit(solution)/shard_map/psum | solution.py:129
  421.8 1.2 convolution_bitcast_fusion.4
  424.5 1.2 convolution_bitcast_fusion.5
  427.2 1.2 convolution_bitcast_fusion.6
  429.2 1.1 convolution_bitcast_fusion.7
  430.8 0.6 copy.56
  432.0 43.5 %reduce-scatter.37.cloned.1.call-done = f32[256,4]{1,0:T(8,128)} async-done(((f32[1024,4]{1,0:T(8,128)}), f32[256,4]{1,0:T(8,128)}) %reduce-scatter.37.cloned.1.call-update) | async-done | bytes 4112
  475.5 1.0 copy.105
  476.5 25.3 %reduce-scatter.33.cloned.1.call-done = f32[256,4]{1,0:T(8,128)} async-done(((f32[1024,4]{1,0:T(8,128)}), f32[256,4]{1,0:T(8,128)}) %reduce-scatter.33.cloned.1.call-update) | async-done | bytes 4112
  501.8 1.0 copy.101
  502.7 25.3 %reduce-scatter.29.cloned.1.call-done = f32[256,4]{1,0:T(8,128)} async-done(((f32[1024,4]{1,0:T(8,128)}), f32[256,4]{1,0:T(8,128)}) %reduce-scatter.29.cloned.1.call-update) | async-done | bytes 4112
  528.1 1.0 copy.97
  529.0 25.2 %reduce-scatter.25.cloned.1.call-done = f32[256,4]{1,0:T(8,128)} async-done(((f32[1024,4]{1,0:T(8,128)}), f32[256,4]{1,0:T(8,128)}) %reduce-scatter.25.cloned.1.call-update) | async-done | bytes 4112
  554.2 1.0 copy.93
  555.5 8.4 %all-reduce.2 = (f32[4]{0:T(128)S(1)}, f32[4]{0:T(128)S(1)}, f32[4]{0:T(128)S(1)}, f32[4]{0:T(128)S(1)}) all-reduce(f32[4]{0:T(128)S(1)} %get-tuple-element.156, f32[4]{0:T(128)S(1)} %get-tuple-element.54, f32[4]{0:T(128)S(1)} %get-tuple-element.154, f32[4]{0:T(128)S(1)} %get-tuple-element.47), channel_id=1, replica_groups=mesh['seq'=64,'tp'=4] {'tp'}, use_global_device_ids=true, to_apply=%region_48.49 | all-reduce | flops 16 | bytes 128 | tf_op jit(solution)/shard_map/psum | solution.py:157
  564.0 10.4 %all_gather.25 = bf16[4,1024]{1,0:T(4,128)(2,1)S(1)} all-gather(bf16[4,256]{1,0:T(4,128)(2,1)S(1)} %get-tuple-element.130), channel_id=1, replica_groups=mesh['seq'=64,'tp'=4] {'tp'}, dimensions={1}, use_global_device_ids=true | all-gather | bytes 10240 | tf_op jit(solution)/shard_map/all_gather | solution.py:162
  574.4 10.4 %all_gather.27 = bf16[4,1024]{1,0:T(4,128)(2,1)S(1)} all-gather(bf16[4,256]{1,0:T(4,128)(2,1)S(1)} %get-tuple-element.131), channel_id=1, replica_groups=mesh['seq'=64,'tp'=4] {'tp'}, dimensions={1}, use_global_device_ids=true | all-gather | bytes 10240 | tf_op jit(solution)/shard_map/all_gather | solution.py:162
  584.8 10.4 %all_gather.29 = bf16[4,1024]{1,0:T(4,128)(2,1)S(1)} all-gather(bf16[4,256]{1,0:T(4,128)(2,1)S(1)} %get-tuple-element.132), channel_id=1, replica_groups=mesh['seq'=64,'tp'=4] {'tp'}, dimensions={1}, use_global_device_ids=true | all-gather | bytes 10240 | tf_op jit(solution)/shard_map/all_gather | solution.py:162
  596.3 4.1 convolution_bitcast_fusion.3
  600.7 4.1 convolution_bitcast_fusion.2
  604.8 4.1 convolution_bitcast_fusion.1
  608.8 10.5 %all_gather.31 = bf16[4,1024]{1,0:T(4,128)(2,1)S(1)} all-gather(bf16[4,256]{1,0:T(4,128)(2,1)S(1)} %get-tuple-element.133), channel_id=1, replica_groups=mesh['seq'=64,'tp'=4] {'tp'}, dimensions={1}, use_global_device_ids=true | all-gather | bytes 10240 | tf_op jit(solution)/shard_map/all_gather | solution.py:162
  620.1 4.1 convolution_bitcast_fusion
  624.2 1.1 reduce-scatter.27.cloned.1.call-done
  625.3 1.0 copy.95
  626.3 25.2 %reduce-scatter.31.cloned.1.call-done = f32[256,4]{1,0:T(8,128)} async-done(((f32[1024,4]{1,0:T(8,128)}), f32[256,4]{1,0:T(8,128)}) %reduce-scatter.31.cloned.1.call-update) | async-done | bytes 4112
  651.5 1.0 copy.99
  652.4 25.3 %reduce-scatter.35.cloned.1.call-done = f32[256,4]{1,0:T(8,128)} async-done(((f32[1024,4]{1,0:T(8,128)}), f32[256,4]{1,0:T(8,128)}) %reduce-scatter.35.cloned.1.call-update) | async-done | bytes 4112
  677.7 1.0 copy.103
  678.7 25.3 %reduce-scatter.39.cloned.1.call-done = f32[256,4]{1,0:T(8,128)} async-done(((f32[1024,4]{1,0:T(8,128)}), f32[256,4]{1,0:T(8,128)}) %reduce-scatter.39.cloned.1.call-update) | async-done | bytes 4112
  704.0 1.0 copy.107
  705.0 0.6 copy.54
  (202 shorter events, 16.8 us)
Async XLA Ops:
  7.2 588.0 %copy-start = (bf16[1024,1024]{1,0:T(8,128)(2,1)S(1)}, bf16[1024,1024]{1,0:T(8,128)(2,1)}, u32[]{:S(2)}) copy-start(bf16[1024,1024]{1,0:T(8,128)(2,1)} %param.26) | copy-start | bytes 6291460
  7.2 49.4 %copy-start.1 = (bf16[1024,256]{1,0:T(8,128)(2,1)S(1)}, bf16[1024,256]{1,0:T(8,128)(2,1)}, u32[]{:S(2)}) copy-start(bf16[1024,256]{1,0:T(8,128)(2,1)} %param.24) | copy-start | bytes 1572868
  7.2 49.6 %copy-start.2 = (bf16[1024,256]{1,0:T(8,128)(2,1)S(1)}, bf16[1024,256]{1,0:T(8,128)(2,1)}, u32[]{:S(2)}) copy-start(bf16[1024,256]{1,0:T(8,128)(2,1)} %param.23) | copy-start | bytes 1572868
  7.2 468.3 %reduce-scatter.37.cloned.1.call-start = ((), (), s32[]{:S(2)}) async-start(), calls=%async_computation.14 | async-start | bytes 655360
  19.2 26.6 %copy-start.3 = (bf16[1024,256]{1,0:T(8,128)(2,1)S(1)}, bf16[1024,256]{1,0:T(8,128)(2,1)}, u32[]{:S(2)}) copy-start(bf16[1024,256]{1,0:T(8,128)(2,1)} %param.22) | copy-start | bytes 1572868
  45.8 22.3 %copy-start.11 = (f32[2,16]{1,0:T(2,128)S(1)}, f32[2,16]{1,0:T(2,128)}, u32[]{:S(2)}) copy-start(f32[2,16]{1,0:T(2,128)} %param.29) | copy-start | bytes 388
  45.8 22.4 %copy-start.14 = (s32[4]{0:T(128)S(1)}, s32[4]{0:T(128)}, u32[]{:S(2)}) copy-start(s32[4]{0:T(128)} %param.35) | copy-start | bytes 52
  45.8 22.4 %copy-start.8 = (s32[4,4]{1,0:T(4,128)S(1)}, s32[4,4]{1,0:T(4,128)}, u32[]{:S(2)}) copy-start(s32[4,4]{1,0:T(4,128)} %param.37) | copy-start | bytes 196
  45.8 22.6 %copy-start.7 = (s32[4,4]{1,0:T(4,128)S(1)}, s32[4,4]{1,0:T(4,128)}, u32[]{:S(2)}) copy-start(s32[4,4]{1,0:T(4,128)} %param.36) | copy-start | bytes 196
  73.3 2.1 copy-start.10
  73.3 2.1 copy-start.13
  73.3 2.2 copy-start.9
  75.4 108.8 %copy-start.5 = (bf16[4,512,256]{1,2,0:T(8,128)(2,1)}, bf16[4,512,256]{1,2,0:T(8,128)(2,1)S(1)}, u32[]{:S(2)}) copy-start(bf16[4,512,256]{1,2,0:T(8,128)(2,1)S(1)} %copy.48) | copy-start | bytes 3145732
  184.6 3.3 copy-start.6
  184.6 237.2 %copy-start.4 = (bf16[256,1024]{1,0:T(8,128)(2,1)S(1)}, bf16[256,1024]{1,0:T(8,128)(2,1)}, u32[]{:S(2)}) copy-start(bf16[256,1024]{1,0:T(8,128)(2,1)} %param.25) | copy-start | bytes 1572868
  423.0 78.7 %reduce-scatter.33.cloned.1.call-start = ((), (), s32[]{:S(2)}) async-start(), calls=%async_computation.12 | async-start | bytes 655360
  425.7 5.1 copy-start.12
  425.7 102.4 %reduce-scatter.29.cloned.1.call-start = ((), (), s32[]{:S(2)}) async-start(), calls=%async_computation.10 | async-start | bytes 655360
  428.4 125.8 %reduce-scatter.25.cloned.1.call-start = ((), (), s32[]{:S(2)}) async-start(), calls=%async_computation.8 | async-start | bytes 655360
  430.3 195.0 %reduce-scatter.27.cloned.1.call-start = ((), (), s32[]{:S(2)}) async-start(), calls=%async_computation.9 | async-start | bytes 655360
  600.5 51.0 %reduce-scatter.31.cloned.1.call-start = ((), (), s32[]{:S(2)}) async-start(), calls=%async_computation.11 | async-start | bytes 655360
  619.3 58.4 %reduce-scatter.35.cloned.1.call-start = ((), (), s32[]{:S(2)}) async-start(), calls=%async_computation.13 | async-start | bytes 655360
  620.1 84.0 %reduce-scatter.39.cloned.1.call-start = ((), (), s32[]{:S(2)}) async-start(), calls=%async_computation.15 | async-start | bytes 655360
Sparse Core Ops, SparseCore 0:
  423.1 52.3 reduce-scatter.36
  478.1 23.6 reduce-scatter.32
  504.3 23.7 reduce-scatter.28
  530.4 23.7 reduce-scatter.24
  600.6 24.6 reduce-scatter.26
  627.7 23.7 reduce-scatter.30
  654.0 23.7 reduce-scatter.34
  680.3 23.7 reduce-scatter.38
where the time goes:
time: 713 us; the launch traced here: 712 us
  blocking collectives  442 us (62%)
  waiting for transfers between devices  196 us (27%)
  matrix products  34.7 us (5%)
  local copies, waits for them, and re-layouts  18.9 us (3%)
  between operations  14.5 us (2%)
    psum x1, blocking collectives, on_device(): lax.psum((local_total * factor, local_sum * jnp.repeat(factor, HEAD_DIM,...  232 us
    unnamed x16, waiting for transfers between devices  196 us
    pmax x1, blocking collectives, on_device(): peak_all = lax.pmax(local_peak, 'seq')  108 us
    all_gather x4, blocking collectives, on_device(): normed = lax.all_gather(normed_local, 'tp', axis=1, tiled=True)  41.7 us
    all_gather x4, blocking collectives, on_device(): normed_two = lax.all_gather(normed_two_local, 'tp', axis=1, tiled=True)  41.6 us
    unnamed x8, matrix products  21 us
  transfers between devices with their start and end apart: 8, of which 8 were waited for; matrix products, arithmetic and copies ran while one was open for 4% of the time, Pallas kernels for 0%

commit v1 on v0

--- a/solution.py
+++ b/solution.py
@@ -91,7 +91,14 @@
         normed_local = (current_local * inverse_rms[:, None] * gain_first_local).astype(
             jnp.bfloat16
         )
-        normed = lax.all_gather(normed_local, "tp", axis=1, tiled=True)
+
+        def open_tables_on_mesh(vec, array_axis):
+            return jnp.concatenate(
+                jax.lax.all_to_all(jnp.stack([vec] * jax.lax.axis_size("tp"), 0), "tp", 0, 0),
+                array_axis,
+            )
+
+        normed = open_tables_on_mesh(normed_local, 1)
         query_full = jnp.dot(normed, query_weight, preferred_element_type=jnp.float32)
         key_full = jnp.dot(normed, key_weight, preferred_element_type=jnp.float32)
         value_full = jnp.dot(normed, value_weight, preferred_element_type=jnp.float32)

time: 713 us -> 719 us (level)
  blocking collectives: 442 us -> 401 us
  starting transfers between devices: 0.51 us -> 15.1 us
  local copies, waits for them, and re-layouts: 18.9 us -> 28.9 us
  waiting for transfers between devices: 196 us -> 206 us
  matrix products: 34.7 us -> 42.7 us
    all_gather x4 -> x0, blocking collectives: 41.7 us -> none  [on_device(): normed = lax.all_gather(normed_local, 'tp', axis=1, tiled=True)]
    all_to_all x0 -> x4, starting transfers between devices: none -> 14.8 us  [open_tables_on_mesh(): jax.lax.all_to_all(jnp.stack([vec] * jax.lax.axis_size('tp'), 0), 'tp', 0...]
    all_to_all x0 -> x4, waiting for transfers between devices: none -> 7.81 us  [open_tables_on_mesh(): jax.lax.all_to_all(jnp.stack([vec] * jax.lax.axis_size('tp'), 0), 'tp', 0...]
    unnamed x43 -> x28, local copies, waits for them, and re-layouts: 12.7 us -> 18.6 us
  transfers between devices with their start and end apart: 8 -> 12, of which waited for: 8 -> 11; matrix products, arithmetic and copies ran while one was open for 4% -> 7% of each run, Pallas kernels for 0% -> 0%
where the time goes in v1:
time: 719 us; the launch traced here: 717 us
  blocking collectives  401 us (56%)
  waiting for transfers between devices  206 us (29%)
  matrix products  42.7 us (6%)
  local copies, waits for them, and re-layouts  28.9 us (4%)
  starting transfers between devices  15.1 us (2%)
  between operations  14.5 us (2%)
  other arithmetic  10 us (1%)
    psum x1, blocking collectives, on_device(): lax.psum((local_total * factor, local_sum * jnp.repeat(factor, HEAD_DIM,...  232 us
    unnamed x16, waiting for transfers between devices  198 us
    pmax x1, blocking collectives, on_device(): peak_all = lax.pmax(local_peak, 'seq')  108 us
    all_gather x4, blocking collectives, on_device(): normed_two = lax.all_gather(normed_two_local, 'tp', axis=1, tiled=True)  41.8 us
    unnamed x8, matrix products  21 us
    unnamed x28, local copies, waits for them, and re-layouts  18.6 us
    all_to_all x4, starting transfers between devices, open_tables_on_mesh(): jax.lax.all_to_all(jnp.stack([vec] * jax.lax.axis_size('tp'), 0), 'tp', 0...  14.8 us
  transfers between devices with their start and end apart: 12, of which 11 were waited for; matrix products, arithmetic and copies ran while one was open for 7% of the time, Pallas kernels for 0%

profile of v1, /device:TPU:8, one launch (start us, length us, event | category | flops | bytes accessed | tf_op | source)
XLA Modules:
  0.0 717.4 jit_solution(16635086544107944688)
XLA Ops:
  8.6 10.5 %all-reduce.3 = (f32[4]{0:T(128)S(1)}, f32[4]{0:T(128)S(1)}, f32[4]{0:T(128)S(1)}, f32[4]{0:T(128)S(1)}) all-reduce(f32[4]{0:T(128)S(1)} %fusion.106, f32[4]{0:T(128)S(1)} %fusion.102, f32[4]{0:T(128)S(1)} %fusion.98, f32[4]{0:T(128)S(1)} %fusion.94), channel_id=1, replica_groups=mesh['seq'=64,'tp'=4] {'tp'}, use_global_device_ids=true, to_apply=%region_38.39 | all-reduce | flops 16 | bytes 128 | tf_op jit(solution)/shard_map/psum | solution.py:89
  20.6 3.2 all-to-all-start.3
  25.6 1.1 slice_reduce_fusion.3
  32.3 2.1 copy.94
  34.4 2.0 copy.97
  37.5 1.5 copy.95
  38.9 2.3 copy.96
  41.9 4.8 all-to-all-start
  46.6 1.3 fusion.182
  47.9 4.0 all-to-all-done
  52.5 3.2 all-to-all-start.2
  55.8 1.3 fusion.173
  57.1 1.4 fusion.174
  58.5 1.4 fusion.183
  59.8 1.2 all-to-all-done.2
  61.7 3.6 all-to-all-start.1
  65.2 1.3 fusion.179
  66.6 1.4 fusion.180
  67.9 2.6 all-to-all-done.1
  70.6 1.4 fusion.176
  72.0 1.4 fusion.177
  73.3 1.4 convolution_convert_fusion
  74.7 1.4 convolution_convert_fusion.1
  80.5 108.2 %all-reduce.1 = (f32[4,4]{1,0:T(4,128)S(1)}, f32[4,4]{1,0:T(4,128)S(1)}, f32[4,4]{1,0:T(4,128)S(1)}, f32[4,4]{1,0:T(4,128)S(1)}) all-reduce(f32[4,4]{1,0:T(4,128)S(1)} %get-tuple-element.78, f32[4,4]{1,0:T(4,128)S(1)} %get-tuple-element.125, f32[4,4]{1,0:T(4,128)S(1)} %get-tuple-element.123, ...), channel_id=1, replica_groups=mesh['seq'=64,'tp'=4] {'seq'}, use_global_device_ids=true, to_apply=%region_40.41 | all-reduce | flops 64 | bytes 512 | tf_op jit(solution)/shard_map/pmax | solution.py:134
  188.9 1.7 fusion.12
  190.6 1.7 fusion.14
  193.8 231.8 %all-reduce = (f32[4,4]{1,0:T(4,128)S(1)}, f32[4,256]{1,0:T(4,128)S(1)}, f32[4,4]{1,0:T(4,128)S(1)}, f32[4,256]{1,0:T(4,128)S(1)}, f32[4,4]{1,0:T(4,128)S(1)}, /...) all-reduce(f32[4,4]{1,0:T(4,128)S(1)} %get-tuple-element.70, ...), channel_id=1, replica_groups=mesh['seq'=64,'tp'=4] {'seq'}, use_global_device_ids=true, to_apply=%region_44.45 | all-reduce | flops 4160 | bytes 33280 | tf_op jit(solution)/shard_map/psum | solution.py:136
  427.8 1.2 convolution_bitcast_fusion.5
  429.2 1.2 convolution_bitcast_fusion.4
  430.9 1.2 convolution_bitcast_fusion.6
  432.6 1.1 convolution_bitcast_fusion.7
  435.8 44.6 %reduce-scatter.33.cloned.1.call-done = f32[256,4]{1,0:T(8,128)} async-done(((f32[1024,4]{1,0:T(8,128)}), f32[256,4]{1,0:T(8,128)}) %reduce-scatter.33.cloned.1.call-update) | async-done | bytes 4112
  481.3 25.3 %reduce-scatter.37.cloned.1.call-done = f32[256,4]{1,0:T(8,128)} async-done(((f32[1024,4]{1,0:T(8,128)}), f32[256,4]{1,0:T(8,128)}) %reduce-scatter.37.cloned.1.call-update) | async-done | bytes 4112
  507.6 25.3 %reduce-scatter.29.cloned.1.call-done = f32[256,4]{1,0:T(8,128)} async-done(((f32[1024,4]{1,0:T(8,128)}), f32[256,4]{1,0:T(8,128)}) %reduce-scatter.29.cloned.1.call-update) | async-done | bytes 4112
  533.9 25.2 %reduce-scatter.25.cloned.1.call-done = f32[256,4]{1,0:T(8,128)} async-done(((f32[1024,4]{1,0:T(8,128)}), f32[256,4]{1,0:T(8,128)}) %reduce-scatter.25.cloned.1.call-update) | async-done | bytes 4112
  560.3 8.4 %all-reduce.2 = (f32[4]{0:T(128)S(1)}, f32[4]{0:T(128)S(1)}, f32[4]{0:T(128)S(1)}, f32[4]{0:T(128)S(1)}) all-reduce(f32[4]{0:T(128)S(1)} %get-tuple-element.158, f32[4]{0:T(128)S(1)} %get-tuple-element.54, f32[4]{0:T(128)S(1)} %get-tuple-element.156, f32[4]{0:T(128)S(1)} %get-tuple-element.47), channel_id=1, replica_groups=mesh['seq'=64,'tp'=4] {'tp'}, use_global_device_ids=true, to_apply=%region_48.49 | all-reduce | flops 16 | bytes 128 | tf_op jit(solution)/shard_map/psum | solution.py:164
  568.9 10.4 %all_gather.12 = bf16[4,1024]{1,0:T(4,128)(2,1)S(1)} all-gather(bf16[4,256]{1,0:T(4,128)(2,1)S(1)} %get-tuple-element.130), channel_id=1, replica_groups=mesh['seq'=64,'tp'=4] {'tp'}, dimensions={1}, use_global_device_ids=true | all-gather | bytes 10240 | tf_op jit(solution)/shard_map/all_gather | solution.py:169
  579.2 10.4 %all_gather.13 = bf16[4,1024]{1,0:T(4,128)(2,1)S(1)} all-gather(bf16[4,256]{1,0:T(4,128)(2,1)S(1)} %get-tuple-element.131), channel_id=1, replica_groups=mesh['seq'=64,'tp'=4] {'tp'}, dimensions={1}, use_global_device_ids=true | all-gather | bytes 10240 | tf_op jit(solution)/shard_map/all_gather | solution.py:169
  589.7 10.5 %all_gather.14 = bf16[4,1024]{1,0:T(4,128)(2,1)S(1)} all-gather(bf16[4,256]{1,0:T(4,128)(2,1)S(1)} %get-tuple-element.132), channel_id=1, replica_groups=mesh['seq'=64,'tp'=4] {'tp'}, dimensions={1}, use_global_device_ids=true | all-gather | bytes 10240 | tf_op jit(solution)/shard_map/all_gather | solution.py:169
  601.4 4.1 convolution_bitcast_fusion.3
  605.6 4.1 convolution_bitcast_fusion.2
  609.6 4.1 convolution_bitcast_fusion.1
  613.7 10.5 %all_gather.15 = bf16[4,1024]{1,0:T(4,128)(2,1)S(1)} all-gather(bf16[4,256]{1,0:T(4,128)(2,1)S(1)} %get-tuple-element.133), channel_id=1, replica_groups=mesh['seq'=64,'tp'=4] {'tp'}, dimensions={1}, use_global_device_ids=true | all-gather | bytes 10240 | tf_op jit(solution)/shard_map/all_gather | solution.py:169
  625.0 4.1 convolution_bitcast_fusion
  629.1 1.2 reduce-scatter.27.cloned.1.call-done
  631.3 25.2 %reduce-scatter.31.cloned.1.call-done = f32[256,4]{1,0:T(8,128)} async-done(((f32[1024,4]{1,0:T(8,128)}), f32[256,4]{1,0:T(8,128)}) %reduce-scatter.31.cloned.1.call-update) | async-done | bytes 4112
  657.4 25.3 %reduce-scatter.35.cloned.1.call-done = f32[256,4]{1,0:T(8,128)} async-done(((f32[1024,4]{1,0:T(8,128)}), f32[256,4]{1,0:T(8,128)}) %reduce-scatter.35.cloned.1.call-update) | async-done | bytes 4112
  683.7 25.3 %reduce-scatter.39.cloned.1.call-done = f32[256,4]{1,0:T(8,128)} async-done(((f32[1024,4]{1,0:T(8,128)}), f32[256,4]{1,0:T(8,128)}) %reduce-scatter.39.cloned.1.call-update) | async-done | bytes 4112
  (197 shorter events, 35.5 us)
Async XLA Ops:
  7.2 593.1 %copy-start = (bf16[1024,1024]{1,0:T(8,128)(2,1)S(1)}, bf16[1024,1024]{1,0:T(8,128)(2,1)}, u32[]{:S(2)}) copy-start(bf16[1024,1024]{1,0:T(8,128)(2,1)} %param.26) | copy-start | bytes 6291460
  7.2 29.2 %copy-start.5 = (bf16[1024,256]{1,0:T(8,128)(2,1)S(1)}, bf16[1024,256]{1,0:T(8,128)(2,1)}, u32[]{:S(2)}) copy-start(bf16[1024,256]{1,0:T(8,128)(2,1)} %param.24) | copy-start | bytes 1572868
  20.6 20.7 %all-to-all-start.3 = ((bf16[4,4,256]{2,1,0:T(4,128)(2,1)}), bf16[4,4,256]{2,1,0:T(4,128)(2,1)S(1)}, u32[]{:S(2)}, u32[]{:S(2)}) async-start(bf16[4,4,256]{2,1,0:T(4,128)(2,1)} %stack.124), calls=%async_computation.3 | async-start | bytes 16384 | tf_op jit(solution)/shard_map/all_to_all | solution.py:97
  41.9 10.1 %all-to-all-start = ((bf16[4,4,256]{2,1,0:T(4,128)(2,1)}), bf16[4,4,256]{2,1,0:T(4,128)(2,1)S(1)}, u32[]{:S(2)}, u32[]{:S(2)}) async-start(bf16[4,4,256]{2,1,0:T(4,128)(2,1)} %stack.50), calls=%async_computation | async-start | bytes 16384 | tf_op jit(solution)/shard_map/all_to_all | solution.py:97
  52.5 8.5 %all-to-all-start.2 = ((bf16[4,4,256]{2,1,0:T(4,128)(2,1)}), bf16[4,4,256]{2,1,0:T(4,128)(2,1)S(1)}, u32[]{:S(2)}, u32[]{:S(2)}) async-start(bf16[4,4,256]{2,1,0:T(4,128)(2,1)} %stack.58), calls=%async_computation.2 | async-start | bytes 16384 | tf_op jit(solution)/shard_map/all_to_all | solution.py:97
  61.7 8.9 %all-to-all-start.1 = ((bf16[4,4,256]{2,1,0:T(4,128)(2,1)}), bf16[4,4,256]{2,1,0:T(4,128)(2,1)S(1)}, u32[]{:S(2)}, u32[]{:S(2)}) async-start(bf16[4,4,256]{2,1,0:T(4,128)(2,1)} %stack.52), calls=%async_computation.1 | async-start | bytes 16384 | tf_op jit(solution)/shard_map/all_to_all | solution.py:97
  65.2 415.1 %reduce-scatter.33.cloned.1.call-start = ((), (), s32[]{:S(2)}) async-start(), calls=%async_computation.16 | async-start | bytes 655360
  70.6 5.5 copy-start.2
  188.7 3.6 copy-start.4
  190.6 236.2 %copy-start.3 = (bf16[1024,256]{0,1:T(8,128)(2,1)S(1)}, bf16[1024,256]{0,1:T(8,128)(2,1)}, u32[]{:S(2)}) copy-start(bf16[1024,256]{0,1:T(8,128)(2,1)} %copy.99) | copy-start | bytes 1572868
  190.6 237.2 %copy-start.1 = (bf16[256,1024]{1,0:T(8,128)(2,1)S(1)}, bf16[256,1024]{1,0:T(8,128)(2,1)}, u32[]{:S(2)}) copy-start(bf16[256,1024]{1,0:T(8,128)(2,1)} %param.25) | copy-start | bytes 1572868
  429.0 77.6 %reduce-scatter.37.cloned.1.call-start = ((), (), s32[]{:S(2)}) async-start(), calls=%async_computation.18 | async-start | bytes 655360
  430.9 102.1 %reduce-scatter.29.cloned.1.call-start = ((), (), s32[]{:S(2)}) async-start(), calls=%async_computation.14 | async-start | bytes 655360
  432.5 126.5 %reduce-scatter.25.cloned.1.call-start = ((), (), s32[]{:S(2)}) async-start(), calls=%async_computation.12 | async-start | bytes 655360
  434.5 195.8 %reduce-scatter.27.cloned.1.call-start = ((), (), s32[]{:S(2)}) async-start(), calls=%async_computation.13 | async-start | bytes 655360
  605.5 50.9 %reduce-scatter.31.cloned.1.call-start = ((), (), s32[]{:S(2)}) async-start(), calls=%async_computation.15 | async-start | bytes 655360
  624.2 58.5 %reduce-scatter.35.cloned.1.call-start = ((), (), s32[]{:S(2)}) async-start(), calls=%async_computation.17 | async-start | bytes 655360
  624.9 84.1 %reduce-scatter.39.cloned.1.call-start = ((), (), s32[]{:S(2)}) async-start(), calls=%async_computation.19 | async-start | bytes 655360
Sparse Core Ops, SparseCore 0:
  429.1 51.1 reduce-scatter.32
  482.9 23.7 reduce-scatter.36
  509.2 23.7 reduce-scatter.28
  535.3 23.7 reduce-scatter.24
  605.6 24.6 reduce-scatter.26
  632.7 23.7 reduce-scatter.30
  658.9 23.7 reduce-scatter.34
  685.2 23.7 reduce-scatter.38
